TPU v7x, 512 devices: a whole 4x8x8 slice. The times are simulated.
512 devices in a mesh: seq: 64 (over z_hi, x, y), tp: 8 (over z_lo, core).
Axes of the slice: x: 4, y: 8, z: 8 (z_hi: 2, z_lo: 4; z = z_hi * 4 + z_lo), core: 2. Of those that a mesh axis runs over, the one named last changes fastest.
Arguments:
- features: bfloat16 [8192, 8192], P('seq', 'tp'), may hold values from -6 to 6
- in_proj: bfloat16 [3, 8192, 1024], P(None, 'seq', 'tp'), may hold values from -0.0625 to 0.0625
- short_taps: float32 [3, 3, 1024], P(None, None, 'tp'), may hold values from -3 to 3
- long_filter: float32 [8192, 1024], P('seq', 'tp'), may hold values from -1.8 to 1.8
- skip_gain: float32 [1024], P('tp'), may hold values from -4 to 4
- out_proj: bfloat16 [1024, 8192], P('tp', 'seq'), may hold values from -0.1875 to 0.1875
Outputs:
- mixed: bfloat16 [8192, 8192], P('seq', 'tp')
All inputs are finite; a program needn't handle non-finite values.
Results may differ from a plain program's by a relative error of at most 0.007.
Values may be sent and summed in bfloat16 or wider, within the bound.
A program may use at most 64 MiB of HBM per device.

v0:
```python
import math
import jax
import jax.numpy as jnp
from jax import lax
from jax.sharding import PartitionSpec as P

HIGHEST = lax.Precision.HIGHEST


def from_behind(array, axis, by):
    count = lax.axis_size(axis)
    pairs = [(i, i + by) for i in range(count) if 0 <= i + by < count]
    return lax.ppermute(array, axis, pairs)


def contract(form, table, values):
    return jnp.einsum(form, table, values, precision=HIGHEST, preferred_element_type=jnp.float32)


def complex_apply(form, tab_real, tab_imag, in_real, in_imag):
    out_real = contract(form, tab_real, in_real) - contract(form, tab_imag, in_imag)
    out_imag = contract(form, tab_real, in_imag) + contract(form, tab_imag, in_real)
    return (out_real, out_imag)


def phases(first, second, modulus, sign):
    product = first[:, None] * second[None, :] % modulus
    angle = sign * 2.0 * math.pi / modulus * product.astype(jnp.float32)
    return (jnp.cos(angle), jnp.sin(angle))


def split_factor(total):
    first_len = 1
    for cand in range(1, total + 1):
        if cand * cand > total:
            break
        if total % cand == 0:
            first_len = cand
    return (first_len, total // first_len)


def local_forward(in_real, in_imag):
    count, tok_rows, chan_dev = in_real.shape
    first_len, second_len = split_factor(tok_rows)
    in_real = in_real.reshape(count, first_len, second_len, chan_dev)
    in_imag = in_imag.reshape(count, first_len, second_len, chan_dev)
    index_first = jnp.arange(first_len, dtype=jnp.int32)
    index_second = jnp.arange(second_len, dtype=jnp.int32)
    tab_real, tab_imag = phases(index_first, index_first, first_len, -1.0)
    mid_real, mid_imag = complex_apply("ma,qabc->qmbc", tab_real, tab_imag, in_real, in_imag)
    turn_real, turn_imag = phases(index_first, index_second, tok_rows, -1.0)
    turn_real = turn_real[None, :, :, None]
    turn_imag = turn_imag[None, :, :, None]
    mid_real, mid_imag = (
        mid_real * turn_real - mid_imag * turn_imag,
        mid_real * turn_imag + mid_imag * turn_real,
    )
    tab_real, tab_imag = phases(index_second, index_second, second_len, -1.0)
    out_real, out_imag = complex_apply("nb,qmbc->qmnc", tab_real, tab_imag, mid_real, mid_imag)
    return (
        out_real.reshape(count, tok_rows, chan_dev),
        out_imag.reshape(count, tok_rows, chan_dev),
    )


def local_inverse(in_real, in_imag):
    count, tok_rows, chan_dev = in_real.shape
    first_len, second_len = split_factor(tok_rows)
    in_real = in_real.reshape(count, first_len, second_len, chan_dev)
    in_imag = in_imag.reshape(count, first_len, second_len, chan_dev)
    index_first = jnp.arange(first_len, dtype=jnp.int32)
    index_second = jnp.arange(second_len, dtype=jnp.int32)
    tab_real, tab_imag = phases(index_second, index_second, second_len, 1.0)
    mid_real, mid_imag = complex_apply("bn,qmnc->qmbc", tab_real, tab_imag, in_real, in_imag)
    turn_real, turn_imag = phases(index_first, index_second, tok_rows, 1.0)
    turn_real = turn_real[None, :, :, None]
    turn_imag = turn_imag[None, :, :, None]
    mid_real, mid_imag = (
        mid_real * turn_real - mid_imag * turn_imag,
        mid_real * turn_imag + mid_imag * turn_real,
    )
    tab_real, tab_imag = phases(index_first, index_first, first_len, 1.0)
    out_real, out_imag = complex_apply("am,qmbc->qabc", tab_real, tab_imag, mid_real, mid_imag)
    return (
        out_real.reshape(count, tok_rows, chan_dev),
        out_imag.reshape(count, tok_rows, chan_dev),
    )


def long_convolve(inner, long_filter):
    tok_rows, chan_dev = inner.shape
    seq_parts = lax.axis_size("seq")
    position = lax.axis_index("seq")
    seq_rows = tok_rows // seq_parts
    freq_count = 2 * seq_parts
    pad_length = 2 * tok_rows * seq_parts
    sent_inner, sent_filter = (
        lax.all_to_all(inner[None], "seq", split_axis=1, concat_axis=0, tiled=True),
        lax.all_to_all(long_filter[None], "seq", split_axis=1, concat_axis=0, tiled=True),
    )
    freq_index = jnp.arange(freq_count, dtype=jnp.int32)
    block_index = jnp.arange(seq_parts, dtype=jnp.int32)
    tab_real, tab_imag = phases(freq_index, block_index, freq_count, -1.0)
    inner_real = contract("qp,prc->qrc", tab_real, sent_inner)
    inner_imag = contract("qp,prc->qrc", tab_imag, sent_inner)
    filter_real = contract("qp,prc->qrc", tab_real, sent_filter)
    filter_imag = contract("qp,prc->qrc", tab_imag, sent_filter)
    global_rows = position * seq_rows + jnp.arange(seq_rows, dtype=jnp.int32)
    turn_real, turn_imag = phases(freq_index, global_rows, pad_length, -1.0)
    turn_real = turn_real[:, :, None]
    turn_imag = turn_imag[:, :, None]
    inner_real, inner_imag = (
        inner_real * turn_real - inner_imag * turn_imag,
        inner_real * turn_imag + inner_imag * turn_real,
    )
    filter_real, filter_imag = (
        filter_real * turn_real - filter_imag * turn_imag,
        filter_real * turn_imag + filter_imag * turn_real,
    )
    inner_real, inner_imag, filter_real, filter_imag = (
        lax.all_to_all(inner_real, "seq", split_axis=0, concat_axis=1, tiled=True),
        lax.all_to_all(inner_imag, "seq", split_axis=0, concat_axis=1, tiled=True),
        lax.all_to_all(filter_real, "seq", split_axis=0, concat_axis=1, tiled=True),
        lax.all_to_all(filter_imag, "seq", split_axis=0, concat_axis=1, tiled=True),
    )
    spec_real, spec_imag = local_forward(
        jnp.concatenate([inner_real, filter_real], 0), jnp.concatenate([inner_imag, filter_imag], 0)
    )
    pair = inner_real.shape[0]
    left_real, right_real = (spec_real[:pair], spec_real[pair:])
    left_imag, right_imag = (spec_imag[:pair], spec_imag[pair:])
    prod_real = left_real * right_real - left_imag * right_imag
    prod_imag = left_real * right_imag + left_imag * right_real
    back_real, back_imag = local_inverse(prod_real, prod_imag)
    back_real, back_imag = (
        lax.all_to_all(back_real, "seq", split_axis=1, concat_axis=0, tiled=True),
        lax.all_to_all(back_imag, "seq", split_axis=1, concat_axis=0, tiled=True),
    )
    back_real, back_imag = (
        back_real * turn_real + back_imag * turn_imag,
        back_imag * turn_real - back_real * turn_imag,
    )
    inv_real, inv_imag = phases(block_index, freq_index, freq_count, 1.0)
    values = (
        contract("pq,qrc->prc", inv_real, back_real) - contract("pq,qrc->prc", inv_imag, back_imag)
    ) / pad_length
    result = lax.all_to_all(values, "seq", split_axis=0, concat_axis=1, tiled=True)
    return result[0]


def per_device(features, in_proj, short_taps, long_filter, skip_gain, out_proj):
    tok_rows = features.shape[0]
    chan_dev = in_proj.shape[2]
    taps_count = short_taps.shape[1]
    full_in = lax.all_gather(in_proj, "seq", axis=1, tiled=True)
    full_out = lax.all_gather(out_proj, "seq", axis=1, tiled=True)
    empty = jnp.zeros((3, tok_rows, chan_dev), jnp.float32)
    piece = jax.tree.map(lambda part: lax.all_gather(part, "tp", axis=1, tiled=True), features)
    weight_rows = lax.slice_in_dim(full_in, 0, piece.shape[1], axis=1)
    projected = (
        empty + jnp.einsum("tk,skc->stc", piece, weight_rows, preferred_element_type=jnp.float32)
    ).astype(jnp.bfloat16)
    earlier = from_behind(projected[:, tok_rows - (taps_count - 1) :, :], "seq", 1)
    padded = jnp.concatenate([earlier, projected], axis=1).astype(jnp.float32)
    filtered = jnp.zeros((3, tok_rows, chan_dev), jnp.float32)
    for offset in range(taps_count):
        begin = taps_count - 1 - offset
        filtered = (
            filtered + short_taps[:, offset, None, :] * padded[:, begin : begin + tok_rows, :]
        )
    query = filtered[0]
    inner = filtered[1] * filtered[2]
    long_mix = long_convolve(inner, long_filter)
    gated = (query * (long_mix + skip_gain[None, :] * inner)).astype(jnp.bfloat16)
    terms = jnp.dot(gated, full_out, preferred_element_type=jnp.float32)
    mixed = lax.psum_scatter(terms, "tp", scatter_dimension=1, tiled=True)
    return mixed.astype(jnp.bfloat16)


def solution(mesh):
    return jax.shard_map(
        per_device,
        mesh=mesh,
        in_specs=(
            P("seq", "tp"),
            P(None, "seq", "tp"),
            P(None, None, "tp"),
            P("seq", "tp"),
            P("tp"),
            P("tp", "seq"),
        ),
        out_specs=P("seq", "tp"),
        check_vma=False,
    )
```

profile of v0, /device:TPU:2, one launch (start us, length us, event | category | flops | bytes accessed | tf_op | source)
XLA Modules:
  0.0 527.9 jit_solution(7247148806284053348)
XLA Ops:
  8.0 19.1 %all-to-all-start.2 = ((f32[1,128,128]{2,0,1:T(1,128)}), f32[1,128,128]{2,0,1:T(1,128)S(1)}, u32[]{:S(2)}, u32[]{:S(2)}) async-start(f32[1,128,128]{2,0,1:T(1,128)} %bitcast.186), calls=%async_computation.2 | async-start | bytes 131072 | tf_op jit(solution)/shard_map/all_to_all | solution.py:99
  27.1 0.8 fusion.242
  28.0 28.7 %all-gather.6.cloned.1.call-done = bf16[128,8192]{1,0:T(8,128)(2,1)} async-done(((bf16[128,1024]{1,0:T(8,128)(2,1)}), bf16[128,8192]{1,0:T(8,128)(2,1)}) %all-gather.6.cloned.1.call-update) | async-done | bytes 2097168 | tf_op jit(solution)/shard_map/all_gather | solution.py:158
  56.6 183.0 %all-gather.4.cloned.1.call-done = bf16[3,8192,128]{2,1,0:T(8,128)(2,1)} async-done(((bf16[3,128,128]{2,1,0:T(8,128)(2,1)}), bf16[3,8192,128]{2,1,0:T(8,128)(2,1)}) %all-gather.4.cloned.1.call-update) | async-done | bytes 6291472 | tf_op jit(solution)/shard_map/all_gather | solution.py:155
  239.6 4.7 fusion.11
  244.3 2.9 collective-permute-start
  247.4 4.5 collective-permute-done
  252.7 7.7 %all-to-all-start = ((f32[1,128,128]{2,0,1:T(1,128)}), f32[1,128,128]{2,0,1:T(1,128)S(1)}, u32[]{:S(2)}, u32[]{:S(2)}) async-start(f32[1,128,128]{2,0,1:T(1,128)} %bitcast.5), calls=%async_computation | async-start | bytes 131072 | tf_op jit(solution)/shard_map/all_to_all | solution.py:98
  260.8 13.2 %all-to-all-done = f32[1,128,128]{2,0,1:T(1,128)S(1)} async-done(((f32[1,128,128]{2,0,1:T(1,128)}), f32[1,128,128]{2,0,1:T(1,128)S(1)}, u32[]{:S(2)}, u32[]{:S(2)}) %all-to-all-start) | async-done | bytes 65568 | tf_op jit(solution)/shard_map/all_to_all | solution.py:98
  275.3 0.8 copy.124
  276.1 5.5 %all-to-all-start.3 = ((f32[128,2,128]{2,1,0:T(2,128)}), f32[128,2,128]{2,1,0:T(2,128)S(1)}, u32[]{:S(2)}, u32[]{:S(2)}) async-start(f32[128,2,128]{2,1,0:T(2,128)} %copy.124), calls=%async_computation.3 | async-start | bytes 262144 | tf_op jit(solution)/shard_map/all_to_all | solution.py:123
  281.6 0.7 copy.130
  282.4 13.2 %all-to-all-done.3 = f32[128,2,128]{2,1,0:T(2,128)S(1)} async-done(((f32[128,2,128]{2,1,0:T(2,128)}), f32[128,2,128]{2,1,0:T(2,128)S(1)}, u32[]{:S(2)}, u32[]{:S(2)}) %all-to-all-start.3) | async-done | bytes 131104 | tf_op jit(solution)/shard_map/all_to_all | solution.py:123
  295.6 5.7 %all-to-all-start.5 = ((f32[128,2,128]{2,1,0:T(2,128)}), f32[128,2,128]{2,1,0:T(2,128)S(1)}, u32[]{:S(2)}, u32[]{:S(2)}) async-start(f32[128,2,128]{2,1,0:T(2,128)} %copy.130), calls=%async_computation.5 | async-start | bytes 262144 | tf_op jit(solution)/shard_map/all_to_all | solution.py:124
  301.3 0.7 copy.128
  302.0 13.2 %all-to-all-done.5 = f32[128,2,128]{2,1,0:T(2,128)S(1)} async-done(((f32[128,2,128]{2,1,0:T(2,128)}), f32[128,2,128]{2,1,0:T(2,128)S(1)}, u32[]{:S(2)}, u32[]{:S(2)}) %all-to-all-start.5) | async-done | bytes 131104 | tf_op jit(solution)/shard_map/all_to_all | solution.py:124
  315.2 5.7 %all-to-all-start.4 = ((f32[128,2,128]{2,1,0:T(2,128)}), f32[128,2,128]{2,1,0:T(2,128)S(1)}, u32[]{:S(2)}, u32[]{:S(2)}) async-start(f32[128,2,128]{2,1,0:T(2,128)} %copy.128), calls=%async_computation.4 | async-start | bytes 262144 | tf_op jit(solution)/shard_map/all_to_all | solution.py:122
  321.8 0.8 copy.120
  322.6 12.3 %all-to-all-done.4 = f32[128,2,128]{2,1,0:T(2,128)S(1)} async-done(((f32[128,2,128]{2,1,0:T(2,128)}), f32[128,2,128]{2,1,0:T(2,128)S(1)}, u32[]{:S(2)}, u32[]{:S(2)}) %all-to-all-start.4) | async-done | bytes 131104 | tf_op jit(solution)/shard_map/all_to_all | solution.py:122
  334.9 5.7 %all-to-all-start.1 = ((f32[128,2,128]{2,1,0:T(2,128)}), f32[128,2,128]{2,1,0:T(2,128)S(1)}, u32[]{:S(2)}, u32[]{:S(2)}) async-start(f32[128,2,128]{2,1,0:T(2,128)} %copy.120), calls=%async_computation.1 | async-start | bytes 262144 | tf_op jit(solution)/shard_map/all_to_all | solution.py:121
  341.0 13.5 %all-to-all-done.1 = f32[128,2,128]{2,1,0:T(2,128)S(1)} async-done(((f32[128,2,128]{2,1,0:T(2,128)}), f32[128,2,128]{2,1,0:T(2,128)S(1)}, u32[]{:S(2)}, u32[]{:S(2)}) %all-to-all-start.1) | async-done | bytes 131104 | tf_op jit(solution)/shard_map/all_to_all | solution.py:121
  360.1 0.7 copy.143
  360.9 5.7 %all-to-all-start.6 = ((f32[2,128,128]{2,0,1:T(2,128)}), f32[2,128,128]{2,0,1:T(2,128)S(1)}, u32[]{:S(2)}, u32[]{:S(2)}) async-start(f32[2,128,128]{2,0,1:T(2,128)} %copy.143), calls=%async_computation.6 | async-start | bytes 262144 | tf_op jit(solution)/shard_map/all_to_all | solution.py:136
  367.3 0.8 copy.149
  368.1 12.5 %all-to-all-done.6 = f32[2,128,128]{2,0,1:T(2,128)S(1)} async-done(((f32[2,128,128]{2,0,1:T(2,128)}), f32[2,128,128]{2,0,1:T(2,128)S(1)}, u32[]{:S(2)}, u32[]{:S(2)}) %all-to-all-start.6) | async-done | bytes 131104 | tf_op jit(solution)/shard_map/all_to_all | solution.py:136
  380.6 5.7 %all-to-all-start.7 = ((f32[2,128,128]{2,0,1:T(2,128)}), f32[2,128,128]{2,0,1:T(2,128)S(1)}, u32[]{:S(2)}, u32[]{:S(2)}) async-start(f32[2,128,128]{2,0,1:T(2,128)} %copy.149), calls=%async_computation.7 | async-start | bytes 262144 | tf_op jit(solution)/shard_map/all_to_all | solution.py:137
  386.5 14.0 %all-to-all-done.7 = f32[2,128,128]{2,0,1:T(2,128)S(1)} async-done(((f32[2,128,128]{2,0,1:T(2,128)}), f32[2,128,128]{2,0,1:T(2,128)S(1)}, u32[]{:S(2)}, u32[]{:S(2)}) %all-to-all-start.7) | async-done | bytes 131104 | tf_op jit(solution)/shard_map/all_to_all | solution.py:137
  402.0 5.7 %all-to-all-start.8 = ((f32[64,2,128]{2,1,0:T(2,128)}), f32[64,2,128]{2,1,0:T(2,128)S(1)}, u32[]{:S(2)}, u32[]{:S(2)}) async-start(f32[64,2,128]{2,1,0:T(2,128)} %copy.152), calls=%async_computation.8 | async-start | bytes 131072 | tf_op jit(solution)/shard_map/all_to_all | solution.py:147
  407.7 54.8 %all-gather.8.cloned.1.call-done = bf16[128,8192]{1,0:T(8,128)(2,1)} async-done(((bf16[128,128]{1,0:T(8,128)(2,1)}), bf16[128,8192]{1,0:T(8,128)(2,1)}) %all-gather.8.cloned.1.call-update) | async-done | bytes 2097168 | tf_op jit(solution)/shard_map/all_gather | solution.py:156
  462.6 4.3 fusion.57
  466.9 52.7 %reduce-scatter.2.cloned.1.call-done = f32[128,1024]{1,0:T(8,128)} async-done(((f32[128,8192]{1,0:T(8,128)}), f32[128,1024]{1,0:T(8,128)}) %reduce-scatter.2.cloned.1.call-update) | async-done | bytes 524304 | tf_op jit(solution)/shard_map/reduce_scatter | solution.py:176
  519.6 1.8 convert_element_type.116
  (63 shorter events, 13.1 us)
Async XLA Ops:
  6.5 50.1 %all-gather.6.cloned.1.call-start = ((), (), s32[]{:S(2)}) async-start(), calls=%async_computation.11 | async-start | bytes 2359296 | tf_op jit(solution)/shard_map/all_gather | solution.py:158
  7.3 232.4 %all-gather.4.cloned.1.call-start = ((), (), s32[]{:S(2)}) async-start(), calls=%async_computation.10 | async-start | bytes 6389760 | tf_op jit(solution)/shard_map/all_gather | solution.py:155
  8.0 244.7 %all-to-all-start.2 = ((f32[1,128,128]{2,0,1:T(1,128)}), f32[1,128,128]{2,0,1:T(1,128)S(1)}, u32[]{:S(2)}, u32[]{:S(2)}) async-start(f32[1,128,128]{2,0,1:T(1,128)} %bitcast.186), calls=%async_computation.2 | async-start | bytes 131072 | tf_op jit(solution)/shard_map/all_to_all | solution.py:99
  244.3 7.6 %collective-permute-start = (bf16[3,2,128]{2,1,0:T(2,128)(2,1)S(1)}, bf16[3,2,128]{2,1,0:T(2,128)(2,1)S(1)}, u32[]{:S(2)}, u32[]{:S(2)}) collective-permute-start(bf16[3,2,128]{2,1,0:T(2,128)(2,1)S(1)} %slice.60), channel_id=1, source_target_pairs={{0,8},{8,16},{16,24},{24,32},{32,40},{40,48},{48,56},{56,64},{64,7... | collective-permute-start | bytes 4616 | tf_op jit(solution)/shard_map/ppermute | solution.py:13
  252.7 21.3 %all-to-all-start = ((f32[1,128,128]{2,0,1:T(1,128)}), f32[1,128,128]{2,0,1:T(1,128)S(1)}, u32[]{:S(2)}, u32[]{:S(2)}) async-start(f32[1,128,128]{2,0,1:T(1,128)} %bitcast.5), calls=%async_computation | async-start | bytes 131072 | tf_op jit(solution)/shard_map/all_to_all | solution.py:98
  276.1 19.5 %all-to-all-start.3 = ((f32[128,2,128]{2,1,0:T(2,128)}), f32[128,2,128]{2,1,0:T(2,128)S(1)}, u32[]{:S(2)}, u32[]{:S(2)}) async-start(f32[128,2,128]{2,1,0:T(2,128)} %copy.124), calls=%async_computation.3 | async-start | bytes 262144 | tf_op jit(solution)/shard_map/all_to_all | solution.py:123
  295.6 19.7 %all-to-all-start.5 = ((f32[128,2,128]{2,1,0:T(2,128)}), f32[128,2,128]{2,1,0:T(2,128)S(1)}, u32[]{:S(2)}, u32[]{:S(2)}) async-start(f32[128,2,128]{2,1,0:T(2,128)} %copy.130), calls=%async_computation.5 | async-start | bytes 262144 | tf_op jit(solution)/shard_map/all_to_all | solution.py:124
  315.2 19.7 %all-to-all-start.4 = ((f32[128,2,128]{2,1,0:T(2,128)}), f32[128,2,128]{2,1,0:T(2,128)S(1)}, u32[]{:S(2)}, u32[]{:S(2)}) async-start(f32[128,2,128]{2,1,0:T(2,128)} %copy.128), calls=%async_computation.4 | async-start | bytes 262144 | tf_op jit(solution)/shard_map/all_to_all | solution.py:122
  321.0 141.6 %all-gather.8.cloned.1.call-start = ((), (), s32[]{:S(2)}) async-start(), calls=%async_computation.12 | async-start | bytes 2129920 | tf_op jit(solution)/shard_map/all_gather | solution.py:156
  334.9 19.7 %all-to-all-start.1 = ((f32[128,2,128]{2,1,0:T(2,128)}), f32[128,2,128]{2,1,0:T(2,128)S(1)}, u32[]{:S(2)}, u32[]{:S(2)}) async-start(f32[128,2,128]{2,1,0:T(2,128)} %copy.120), calls=%async_computation.1 | async-start | bytes 262144 | tf_op jit(solution)/shard_map/all_to_all | solution.py:121
  360.1 102.5 %copy-start = (f32[128]{0:T(128)S(1)}, f32[128]{0:T(128)}, u32[]{:S(2)}) copy-start(f32[128]{0:T(128)} %param.10) | copy-start | bytes 1540
  360.9 19.7 %all-to-all-start.6 = ((f32[2,128,128]{2,0,1:T(2,128)}), f32[2,128,128]{2,0,1:T(2,128)S(1)}, u32[]{:S(2)}, u32[]{:S(2)}) async-start(f32[2,128,128]{2,0,1:T(2,128)} %copy.143), calls=%async_computation.6 | async-start | bytes 262144 | tf_op jit(solution)/shard_map/all_to_all | solution.py:136
  380.6 19.8 %all-to-all-start.7 = ((f32[2,128,128]{2,0,1:T(2,128)}), f32[2,128,128]{2,0,1:T(2,128)S(1)}, u32[]{:S(2)}, u32[]{:S(2)}) async-start(f32[2,128,128]{2,0,1:T(2,128)} %copy.149), calls=%async_computation.7 | async-start | bytes 262144 | tf_op jit(solution)/shard_map/all_to_all | solution.py:137
  402.0 60.6 %all-to-all-start.8 = ((f32[64,2,128]{2,1,0:T(2,128)}), f32[64,2,128]{2,1,0:T(2,128)S(1)}, u32[]{:S(2)}, u32[]{:S(2)}) async-start(f32[64,2,128]{2,1,0:T(2,128)} %copy.152), calls=%async_computation.8 | async-start | bytes 131072 | tf_op jit(solution)/shard_map/all_to_all | solution.py:147
  407.7 111.9 %reduce-scatter.2.cloned.1.call-start = ((), (), s32[]{:S(2)}) async-start(), calls=%async_computation.13 | async-start | bytes 4718592 | tf_op jit(solution)/shard_map/reduce_scatter | solution.py:176
Sparse Core Ops, SparseCore 0:
  9.4 47.1 all-gather.5
  61.0 178.5 all-gather.3
  326.1 136.4 all-gather.7
  467.0 52.4 reduce-scatter.1
where the time goes:
time: 529 us; the launch traced here: 528 us
  waiting for transfers between devices  418 us (79%)
  starting transfers between devices  69.7 us (13%)
  matrix products  17.3 us (3%)
  between operations  13.5 us (3%)
  local copies, waits for them, and re-layouts  6.82 us (1%)
    all_gather x1, waiting for transfers between devices, per_device(): full_in = lax.all_gather(in_proj, 'seq', axis=1, tiled=True)  183 us
    all_gather x1, waiting for transfers between devices, per_device(): full_out = lax.all_gather(out_proj, 'seq', axis=1, tiled=True)  54.8 us
    reduce_scatter x1, waiting for transfers between devices, per_device(): mixed = lax.psum_scatter(terms, 'tp', scatter_dimension=1, tiled=True)  52.7 us
    all_gather x1, waiting for transfers between devices, per_device(): lax.all_gather(part, 'tp', axis=1, tiled=True)  28.7 us
    all_to_all x1, starting transfers between devices, long_convolve(): lax.all_to_all(long_filter[None], 'seq', split_axis=1, concat_axis=0, til...  19.1 us
    all_to_all x1, waiting for transfers between devices, long_convolve(): lax.all_to_all(back_imag, 'seq', split_axis=1, concat_axis=0, tiled=True)  14 us
    all_to_all x1, waiting for transfers between devices, long_convolve(): lax.all_to_all(inner_real, 'seq', split_axis=0, concat_axis=1, tiled=True)  13.5 us
    all_to_all x1, waiting for transfers between devices, long_convolve(): lax.all_to_all(filter_real, 'seq', split_axis=0, concat_axis=1, tiled=True)  13.2 us
  transfers between devices with their start and end apart: 14, of which 12 were waited for; matrix products, arithmetic and copies ran while one was open for 4% of the time, Pallas kernels for 0%

commit v1 on v0

--- a/solution.py
+++ b/solution.py
@@ -152,7 +152,14 @@
     tok_rows = features.shape[0]
     chan_dev = in_proj.shape[2]
     taps_count = short_taps.shape[1]
-    full_in = lax.all_gather(in_proj, "seq", axis=1, tiled=True)
+
+    def heaps_test(local_array, ax_name):
+        v_now = jax.lax.all_to_all(
+            jnp.stack([local_array] * jax.lax.axis_size(ax_name), axis=0), ax_name, 0, 0
+        )
+        return jnp.concatenate(v_now, axis=1)
+
+    full_in = heaps_test(in_proj, "seq")
     full_out = lax.all_gather(out_proj, "seq", axis=1, tiled=True)
     empty = jnp.zeros((3, tok_rows, chan_dev), jnp.float32)
     piece = jax.tree.map(lambda part: lax.all_gather(part, "tp", axis=1, tiled=True), features)

time: 529 us -> 501 us (0.947)
  waiting for transfers between devices: 418 us -> 356 us
  starting transfers between devices: 69.7 us -> 89.5 us
  local copies, waits for them, and re-layouts: 6.82 us -> 19.2 us
    all_gather x1 -> x0, waiting for transfers between devices: 183 us -> none  [per_device(): full_in = lax.all_gather(in_proj, 'seq', axis=1, tiled=True)]
    all_to_all x0 -> x1, waiting for transfers between devices: none -> 171 us  [heaps_test(): jax.lax.all_to_all(jnp.stack([local_array] * jax.lax.axis_size(ax_name),...]
    all_gather x1, waiting for transfers between devices: 28.7 us -> 0.01 us  [per_device(): lax.all_gather(part, 'tp', axis=1, tiled=True)]
    all_to_all x0 -> x1, starting transfers between devices: none -> 19.4 us  [heaps_test(): jax.lax.all_to_all(jnp.stack([local_array] * jax.lax.axis_size(ax_name),...]
    all_gather x1, waiting for transfers between devices: 54.8 us -> 35.9 us  [per_device(): full_out = lax.all_gather(out_proj, 'seq', axis=1, tiled=True)]
    reshape x0 -> x1, local copies, waits for them, and re-layouts: none -> 8.05 us  [heaps_test(): return jnp.concatenate(v_now, axis=1)]
    all_to_all x1, starting transfers between devices: 19.1 us -> 12 us  [long_convolve(): lax.all_to_all(long_filter[None], 'seq', split_axis=1, concat_axis=0, til...]
    all_to_all x1, starting transfers between devices: 7.69 us -> 14.3 us  [long_convolve(): lax.all_to_all(inner[None], 'seq', split_axis=1, concat_axis=0, tiled=True)]
  transfers between devices with their start and end apart: 14 -> 14, of which waited for: 12 -> 11; matrix products, arithmetic and copies ran while one was open for 4% -> 5% of each run, Pallas kernels for 0% -> 0%
where the time goes in v1:
time: 501 us; the launch traced here: 500 us
  waiting for transfers between devices  356 us (71%)
  starting transfers between devices  89.5 us (18%)
  local copies, waits for them, and re-layouts  19.2 us (4%)
  matrix products  17.3 us (3%)
  between operations  15.3 us (3%)
    all_to_all x1, waiting for transfers between devices, heaps_test(): jax.lax.all_to_all(jnp.stack([local_array] * jax.lax.axis_size(ax_name),...  171 us
    reduce_scatter x1, waiting for transfers between devices, per_device(): mixed = lax.psum_scatter(terms, 'tp', scatter_dimension=1, tiled=True)  52.7 us
    all_gather x1, waiting for transfers between devices, per_device(): full_out = lax.all_gather(out_proj, 'seq', axis=1, tiled=True)  35.9 us
    all_to_all x1, starting transfers between devices, heaps_test(): jax.lax.all_to_all(jnp.stack([local_array] * jax.lax.axis_size(ax_name),...  19.4 us
    all_to_all x1, starting transfers between devices, long_convolve(): lax.all_to_all(inner[None], 'seq', split_axis=1, concat_axis=0, tiled=True)  14.3 us
    all_to_all x1, waiting for transfers between devices, long_convolve(): lax.all_to_all(back_imag, 'seq', split_axis=1, concat_axis=0, tiled=True)  13.8 us
    all_to_all x1, waiting for transfers between devices, long_convolve(): lax.all_to_all(filter_real, 'seq', split_axis=0, concat_axis=1, tiled=True)  13.7 us
    all_to_all x1, waiting for transfers between devices, long_convolve(): lax.all_to_all(inner_imag, 'seq', split_axis=0, concat_axis=1, tiled=True)  13.2 us
  transfers between devices with their start and end apart: 14, of which 11 were waited for; matrix products, arithmetic and copies ran while one was open for 5% of the time, Pallas kernels for 0%

profile of v1, /device:TPU:2, one launch (start us, length us, event | category | flops | bytes accessed | tf_op | source)
XLA Modules:
  0.0 500.5 jit_solution(646098106519660933)
XLA Ops:
  7.4 5.1 %stack.2 = bf16[64,3,128,128]{3,2,1,0:T(8,128)(2,1)} broadcast(bf16[3,128,128]{2,1,0:T(8,128)(2,1)} %param.7), dimensions={1,2,3} | broadcast | bytes 6389760 | tf_op jit(solution)/shard_map/stack | solution.py:158
  12.5 19.4 %all-to-all-start = ((bf16[64,3,128,128]{3,2,1,0:T(8,128)(2,1)}), bf16[64,3,128,128]{3,2,1,0:T(8,128)(2,1)}, u32[]{:S(2)}, u32[]{:S(2)}) async-start(bf16[64,3,128,128]{3,2,1,0:T(8,128)(2,1)} %stack.2), calls=%async_computation | async-start | bytes 12582912 | tf_op jit(solution)/shard_map/all_to_all | solution.py:157
  32.7 170.6 %all-to-all-done = bf16[64,3,128,128]{3,2,1,0:T(8,128)(2,1)} async-done(((bf16[64,3,128,128]{3,2,1,0:T(8,128)(2,1)}), bf16[64,3,128,128]{3,2,1,0:T(8,128)(2,1)}, u32[]{:S(2)}, u32[]{:S(2)}) %all-to-all-start) | async-done | bytes 6291488 | tf_op jit(solution)/shard_map/all_to_all | solution.py:157
  203.2 12.0 %all-to-all-start.3 = ((f32[1,128,128]{2,0,1:T(1,128)}), f32[1,128,128]{2,0,1:T(1,128)S(1)}, u32[]{:S(2)}, u32[]{:S(2)}) async-start(f32[1,128,128]{2,0,1:T(1,128)} %bitcast.13), calls=%async_computation.3 | async-start | bytes 131072 | tf_op jit(solution)/shard_map/all_to_all | solution.py:99
  215.2 8.1 %copy.119 = bf16[3,64,128,128]{3,2,1,0:T(8,128)(2,1)} copy(bf16[3,64,128,128]{3,2,0,1:T(8,128)(2,1)} %bitcast) | data formatting | bytes 12582912 | tf_op jit(solution)/shard_map/reshape | solution.py:160
  223.2 4.7 fusion.11
  227.9 3.4 collective-permute-start
  231.5 4.1 collective-permute-done
  236.3 14.3 %all-to-all-start.1 = ((f32[1,128,128]{2,0,1:T(1,128)}), f32[1,128,128]{2,0,1:T(1,128)S(1)}, u32[]{:S(2)}, u32[]{:S(2)}) async-start(f32[1,128,128]{2,0,1:T(1,128)} %bitcast.7), calls=%async_computation.1 | async-start | bytes 131072 | tf_op jit(solution)/shard_map/all_to_all | solution.py:98
  251.0 13.2 %all-to-all-done.1 = f32[1,128,128]{2,0,1:T(1,128)S(1)} async-done(((f32[1,128,128]{2,0,1:T(1,128)}), f32[1,128,128]{2,0,1:T(1,128)S(1)}, u32[]{:S(2)}, u32[]{:S(2)}) %all-to-all-start.1) | async-done | bytes 65568 | tf_op jit(solution)/shard_map/all_to_all | solution.py:98
  265.6 0.8 copy.131
  266.3 5.5 %all-to-all-start.5 = ((f32[128,2,128]{2,1,0:T(2,128)}), f32[128,2,128]{2,1,0:T(2,128)S(1)}, u32[]{:S(2)}, u32[]{:S(2)}) async-start(f32[128,2,128]{2,1,0:T(2,128)} %copy.131), calls=%async_computation.5 | async-start | bytes 262144 | tf_op jit(solution)/shard_map/all_to_all | solution.py:122
  271.9 0.7 copy.133
  272.6 13.2 %all-to-all-done.5 = f32[128,2,128]{2,1,0:T(2,128)S(1)} async-done(((f32[128,2,128]{2,1,0:T(2,128)}), f32[128,2,128]{2,1,0:T(2,128)S(1)}, u32[]{:S(2)}, u32[]{:S(2)}) %all-to-all-start.5) | async-done | bytes 131104 | tf_op jit(solution)/shard_map/all_to_all | solution.py:122
  285.8 5.7 %all-to-all-start.6 = ((f32[128,2,128]{2,1,0:T(2,128)}), f32[128,2,128]{2,1,0:T(2,128)S(1)}, u32[]{:S(2)}, u32[]{:S(2)}) async-start(f32[128,2,128]{2,1,0:T(2,128)} %copy.133), calls=%async_computation.6 | async-start | bytes 262144 | tf_op jit(solution)/shard_map/all_to_all | solution.py:124
  292.1 0.8 copy.123
  292.9 12.6 %all-to-all-done.6 = f32[128,2,128]{2,1,0:T(2,128)S(1)} async-done(((f32[128,2,128]{2,1,0:T(2,128)}), f32[128,2,128]{2,1,0:T(2,128)S(1)}, u32[]{:S(2)}, u32[]{:S(2)}) %all-to-all-start.6) | async-done | bytes 131104 | tf_op jit(solution)/shard_map/all_to_all | solution.py:124
  305.5 5.7 %all-to-all-start.2 = ((f32[128,2,128]{2,1,0:T(2,128)}), f32[128,2,128]{2,1,0:T(2,128)S(1)}, u32[]{:S(2)}, u32[]{:S(2)}) async-start(f32[128,2,128]{2,1,0:T(2,128)} %copy.123), calls=%async_computation.2 | async-start | bytes 262144 | tf_op jit(solution)/shard_map/all_to_all | solution.py:121
  311.5 0.8 copy.127
  312.3 12.8 %all-to-all-done.2 = f32[128,2,128]{2,1,0:T(2,128)S(1)} async-done(((f32[128,2,128]{2,1,0:T(2,128)}), f32[128,2,128]{2,1,0:T(2,128)S(1)}, u32[]{:S(2)}, u32[]{:S(2)}) %all-to-all-start.2) | async-done | bytes 131104 | tf_op jit(solution)/shard_map/all_to_all | solution.py:121
  325.1 5.7 %all-to-all-start.4 = ((f32[128,2,128]{2,1,0:T(2,128)}), f32[128,2,128]{2,1,0:T(2,128)S(1)}, u32[]{:S(2)}, u32[]{:S(2)}) async-start(f32[128,2,128]{2,1,0:T(2,128)} %copy.127), calls=%async_computation.4 | async-start | bytes 262144 | tf_op jit(solution)/shard_map/all_to_all | solution.py:123
  331.1 13.7 %all-to-all-done.4 = f32[128,2,128]{2,1,0:T(2,128)S(1)} async-done(((f32[128,2,128]{2,1,0:T(2,128)}), f32[128,2,128]{2,1,0:T(2,128)S(1)}, u32[]{:S(2)}, u32[]{:S(2)}) %all-to-all-start.4) | async-done | bytes 131104 | tf_op jit(solution)/shard_map/all_to_all | solution.py:123
  351.1 6.0 %all-to-all-start.7 = ((f32[2,128,128]{2,0,1:T(2,128)}), f32[2,128,128]{2,0,1:T(2,128)S(1)}, u32[]{:S(2)}, u32[]{:S(2)}) async-start(f32[2,128,128]{2,0,1:T(2,128)} %copy.146), calls=%async_computation.7 | async-start | bytes 262144 | tf_op jit(solution)/shard_map/all_to_all | solution.py:136
  357.7 0.8 copy.152
  358.5 12.5 %all-to-all-done.7 = f32[2,128,128]{2,0,1:T(2,128)S(1)} async-done(((f32[2,128,128]{2,0,1:T(2,128)}), f32[2,128,128]{2,0,1:T(2,128)S(1)}, u32[]{:S(2)}, u32[]{:S(2)}) %all-to-all-start.7) | async-done | bytes 131104 | tf_op jit(solution)/shard_map/all_to_all | solution.py:136
  371.0 6.0 %all-to-all-start.8 = ((f32[2,128,128]{2,0,1:T(2,128)}), f32[2,128,128]{2,0,1:T(2,128)S(1)}, u32[]{:S(2)}, u32[]{:S(2)}) async-start(f32[2,128,128]{2,0,1:T(2,128)} %copy.152), calls=%async_computation.8 | async-start | bytes 262144 | tf_op jit(solution)/shard_map/all_to_all | solution.py:137
  377.1 13.8 %all-to-all-done.8 = f32[2,128,128]{2,0,1:T(2,128)S(1)} async-done(((f32[2,128,128]{2,0,1:T(2,128)}), f32[2,128,128]{2,0,1:T(2,128)S(1)}, u32[]{:S(2)}, u32[]{:S(2)}) %all-to-all-start.8) | async-done | bytes 131104 | tf_op jit(solution)/shard_map/all_to_all | solution.py:137
  392.5 5.7 %all-to-all-start.9 = ((f32[64,2,128]{2,1,0:T(2,128)}), f32[64,2,128]{2,1,0:T(2,128)S(1)}, u32[]{:S(2)}, u32[]{:S(2)}) async-start(f32[64,2,128]{2,1,0:T(2,128)} %copy.155), calls=%async_computation.9 | async-start | bytes 131072 | tf_op jit(solution)/shard_map/all_to_all | solution.py:147
  398.3 35.9 %all-gather.5.cloned.1.call-done = bf16[128,8192]{1,0:T(8,128)(2,1)} async-done(((bf16[128,128]{1,0:T(8,128)(2,1)}), bf16[128,8192]{1,0:T(8,128)(2,1)}) %all-gather.5.cloned.1.call-update) | async-done | bytes 2097168 | tf_op jit(solution)/shard_map/all_gather | solution.py:163
  434.2 4.3 fusion.57
  438.6 52.7 %reduce-scatter.2.cloned.1.call-done = f32[128,1024]{1,0:T(8,128)} async-done(((f32[128,8192]{1,0:T(8,128)}), f32[128,1024]{1,0:T(8,128)}) %reduce-scatter.2.cloned.1.call-update) | async-done | bytes 524304 | tf_op jit(solution)/shard_map/reduce_scatter | solution.py:183
  491.3 1.8 convert_element_type.116
  (66 shorter events, 13.0 us)
Async XLA Ops:
  12.5 20.2 %copy-start = (f32[3,3,128]{2,1,0:T(4,128)S(1)}, f32[3,3,128]{2,1,0:T(4,128)}, u32[]{:S(2)}) copy-start(f32[3,3,128]{2,1,0:T(4,128)} %param.8) | copy-start | bytes 13828
  12.5 190.7 %all-to-all-start = ((bf16[64,3,128,128]{3,2,1,0:T(8,128)(2,1)}), bf16[64,3,128,128]{3,2,1,0:T(8,128)(2,1)}, u32[]{:S(2)}, u32[]{:S(2)}) async-start(bf16[64,3,128,128]{3,2,1,0:T(8,128)(2,1)} %stack.2), calls=%async_computation | async-start | bytes 12582912 | tf_op jit(solution)/shard_map/all_to_all | solution.py:157
  31.9 191.4 %all-gather.3.cloned.1.call-start = ((), (), s32[]{:S(2)}) async-start(), calls=%async_computation.11 | async-start | bytes 2359296 | tf_op jit(solution)/shard_map/all_gather | solution.py:165
  203.2 33.0 %all-to-all-start.3 = ((f32[1,128,128]{2,0,1:T(1,128)}), f32[1,128,128]{2,0,1:T(1,128)S(1)}, u32[]{:S(2)}, u32[]{:S(2)}) async-start(f32[1,128,128]{2,0,1:T(1,128)} %bitcast.13), calls=%async_computation.3 | async-start | bytes 131072 | tf_op jit(solution)/shard_map/all_to_all | solution.py:99
  227.9 7.6 %collective-permute-start = (bf16[3,2,128]{2,1,0:T(2,128)(2,1)S(1)}, bf16[3,2,128]{2,1,0:T(2,128)(2,1)S(1)}, u32[]{:S(2)}, u32[]{:S(2)}) collective-permute-start(bf16[3,2,128]{2,1,0:T(2,128)(2,1)S(1)} %slice.60), channel_id=1, source_target_pairs={{0,8},{8,16},{16,24},{24,32},{32,40},{40,48},{48,56},{56,64},{64,7... | collective-permute-start | bytes 4616 | tf_op jit(solution)/shard_map/ppermute | solution.py:13
  236.3 27.9 %all-to-all-start.1 = ((f32[1,128,128]{2,0,1:T(1,128)}), f32[1,128,128]{2,0,1:T(1,128)S(1)}, u32[]{:S(2)}, u32[]{:S(2)}) async-start(f32[1,128,128]{2,0,1:T(1,128)} %bitcast.7), calls=%async_computation.1 | async-start | bytes 131072 | tf_op jit(solution)/shard_map/all_to_all | solution.py:98
  266.3 19.5 %all-to-all-start.5 = ((f32[128,2,128]{2,1,0:T(2,128)}), f32[128,2,128]{2,1,0:T(2,128)S(1)}, u32[]{:S(2)}, u32[]{:S(2)}) async-start(f32[128,2,128]{2,1,0:T(2,128)} %copy.131), calls=%async_computation.5 | async-start | bytes 262144 | tf_op jit(solution)/shard_map/all_to_all | solution.py:122
  285.8 19.7 %all-to-all-start.6 = ((f32[128,2,128]{2,1,0:T(2,128)}), f32[128,2,128]{2,1,0:T(2,128)S(1)}, u32[]{:S(2)}, u32[]{:S(2)}) async-start(f32[128,2,128]{2,1,0:T(2,128)} %copy.133), calls=%async_computation.6 | async-start | bytes 262144 | tf_op jit(solution)/shard_map/all_to_all | solution.py:124
  291.5 142.7 %all-gather.5.cloned.1.call-start = ((), (), s32[]{:S(2)}) async-start(), calls=%async_computation.12 | async-start | bytes 2129920 | tf_op jit(solution)/shard_map/all_gather | solution.py:163
  305.5 19.7 %all-to-all-start.2 = ((f32[128,2,128]{2,1,0:T(2,128)}), f32[128,2,128]{2,1,0:T(2,128)S(1)}, u32[]{:S(2)}, u32[]{:S(2)}) async-start(f32[128,2,128]{2,1,0:T(2,128)} %copy.123), calls=%async_computation.2 | async-start | bytes 262144 | tf_op jit(solution)/shard_map/all_to_all | solution.py:121
  325.1 19.7 %all-to-all-start.4 = ((f32[128,2,128]{2,1,0:T(2,128)}), f32[128,2,128]{2,1,0:T(2,128)S(1)}, u32[]{:S(2)}, u32[]{:S(2)}) async-start(f32[128,2,128]{2,1,0:T(2,128)} %copy.127), calls=%async_computation.4 | async-start | bytes 262144 | tf_op jit(solution)/shard_map/all_to_all | solution.py:123
  347.9 86.3 %copy-start.1 = (f32[128]{0:T(128)S(1)}, f32[128]{0:T(128)}, u32[]{:S(2)}) copy-start(f32[128]{0:T(128)} %param.10) | copy-start | bytes 1540
  351.1 19.9 %all-to-all-start.7 = ((f32[2,128,128]{2,0,1:T(2,128)}), f32[2,128,128]{2,0,1:T(2,128)S(1)}, u32[]{:S(2)}, u32[]{:S(2)}) async-start(f32[2,128,128]{2,0,1:T(2,128)} %copy.146), calls=%async_computation.7 | async-start | bytes 262144 | tf_op jit(solution)/shard_map/all_to_all | solution.py:136
  371.0 19.9 %all-to-all-start.8 = ((f32[2,128,128]{2,0,1:T(2,128)}), f32[2,128,128]{2,0,1:T(2,128)S(1)}, u32[]{:S(2)}, u32[]{:S(2)}) async-start(f32[2,128,128]{2,0,1:T(2,128)} %copy.152), calls=%async_computation.8 | async-start | bytes 262144 | tf_op jit(solution)/shard_map/all_to_all | solution.py:137
  392.5 41.7 %all-to-all-start.9 = ((f32[64,2,128]{2,1,0:T(2,128)}), f32[64,2,128]{2,1,0:T(2,128)S(1)}, u32[]{:S(2)}, u32[]{:S(2)}) async-start(f32[64,2,128]{2,1,0:T(2,128)} %copy.155), calls=%async_computation.9 | async-start | bytes 131072 | tf_op jit(solution)/shard_map/all_to_all | solution.py:147
  398.3 93.0 %reduce-scatter.2.cloned.1.call-start = ((), (), s32[]{:S(2)}) async-start(), calls=%async_computation.13 | async-start | bytes 4718592 | tf_op jit(solution)/shard_map/reduce_scatter | solution.py:183
Sparse Core Ops, SparseCore 0:
  34.8 156.9 all-gather.2
  438.7 52.5 reduce-scatter.1
Sparse Core Ops, SparseCore 1:
  296.3 137.9 all-gather.4
